TPU v7x, 256 devices: a whole 4x4x8 slice. The times are simulated.
256 devices in a mesh: dp: 8 (over z_hi, x), expert: 32 (over z_lo, y, core).
Axes of the slice: x: 4, y: 4, z: 8 (z_hi: 2, z_lo: 4; z = z_hi * 4 + z_lo), core: 2. Of those that a mesh axis runs over, the one named last changes fastest.
Arguments:
- tokens: bfloat16 [8192, 7168], P('expert', 'dp'), may hold values from -6 to 6
- cotangent: bfloat16 [8192, 7168], P('expert', 'dp'), may hold values from -6 to 6
- routing: int32 [8192, 8], P('expert'), may hold values from 0 to 255, as said below
- gate_values: float32 [8192, 8], P('expert'), may hold values from 0.05 to 0.6
- hidden_weight: bfloat16 [32, 7168, 2048], P('expert', 'dp'), may hold values from -0.0625 to 0.0625
- output_weight: bfloat16 [32, 1024, 7168], P('expert', None, 'dp'), may hold values from -0.1875 to 0.1875
Outputs:
- mixed: bfloat16 [8192, 7168], P('expert', 'dp')
- token_grad: bfloat16 [8192, 7168], P('expert', 'dp')
- hidden_grad: bfloat16 [32, 7168, 2048], P('expert', 'dp')
- output_grad: bfloat16 [32, 1024, 7168], P('expert', None, 'dp')
Inputs may be any that keep to these rules, and one draw needn't show every extreme that they name: `routing`: each row names 8 different experts. Within the 256 rows of one index of expert no expert is named by more than 16 rows, and in every such block some experts below 32 are named by exactly 16 rows.
All inputs are finite; a program needn't handle non-finite values.
Results may differ from a plain program's by a relative error of at most 0.022.
Values may be sent and summed in bfloat16 or wider, within the bound.
A program may use at most 64 MiB of HBM per device.

v0:
```python
import jax
import jax.numpy as jnp
from jax import lax
from jax.sharding import PartitionSpec as P

ROUTED = 256


def slot_table(routing_block, gate_block, expert_count, slot_count):
    tok_count = routing_block.shape[0]
    picked = routing_block.reshape(-1)
    onehot = (picked[:, None] == jnp.arange(expert_count, dtype=jnp.int32)[None, :]).astype(
        jnp.int32
    )
    earlier = jnp.cumsum(onehot, axis=0) - onehot
    ranking = jnp.sum(earlier * onehot, axis=1)
    slot_index = (picked * slot_count + ranking).reshape(tok_count, -1)
    target = jnp.arange(expert_count * slot_count, dtype=jnp.int32)
    matched = slot_index[None, :, :] == target[:, None, None]
    placed = jnp.any(matched, axis=2).astype(jnp.float32)
    gate_slot = jnp.sum(
        jnp.where(matched, gate_block[None, :, :], jnp.zeros_like(gate_block)[None, :, :]),
        axis=(1, 2),
    )
    return (placed, gate_slot)


def activate(hidden, half_width):
    gate_part = hidden[:, :half_width]
    up_part = hidden[:, half_width:]
    return (gate_part * jax.nn.sigmoid(gate_part) * up_part).astype(jnp.bfloat16)


def activate_grad(hidden, act_grad, half_width):
    gate_part = hidden[:, :half_width]
    up_part = hidden[:, half_width:]
    sigmoid_gate = jax.nn.sigmoid(gate_part)
    gate_grad = act_grad * up_part * sigmoid_gate * (1.0 + gate_part * (1.0 - sigmoid_gate))
    up_grad = act_grad * gate_part * sigmoid_gate
    return jnp.concatenate([gate_grad, up_grad], axis=1).astype(jnp.bfloat16)


def body(tokens, cotangent, routing, gate_values, hidden_weight, output_weight):
    tok_count, column_width = tokens.shape
    pick_count = routing.shape[1]
    expert_count = lax.axis_size("expert")
    slot_count = 2 * tok_count * pick_count // ROUTED
    row_total = expert_count * slot_count
    contract_cols = (((1,), (1,)), ((), ()))
    contract_rows = (((0,), (0,)), ((), ()))
    placed, gate_slot = slot_table(routing, gate_values, expert_count, slot_count)
    placed_half = placed.astype(jnp.bfloat16)
    send_shape = (expert_count, slot_count, column_width)
    token_rows = (
        jnp.dot(placed_half, tokens, preferred_element_type=jnp.float32)
        .astype(jnp.bfloat16)
        .reshape(send_shape)
    )
    cot_rows = (
        (gate_slot[:, None] * jnp.dot(placed_half, cotangent, preferred_element_type=jnp.float32))
        .astype(jnp.bfloat16)
        .reshape(send_shape)
    )
    inner_weight = hidden_weight[0]
    outer_weight = output_weight[0]
    half_width = outer_weight.shape[0]
    arrived = (
        lax.all_to_all(token_rows, "expert", split_axis=0, concat_axis=0, tiled=True),
        lax.all_to_all(cot_rows, "expert", split_axis=0, concat_axis=0, tiled=True),
    )
    expert_rows = arrived[0].reshape(row_total, column_width)
    scaled_cot = arrived[1].reshape(row_total, column_width)
    partial_hidden = jnp.dot(expert_rows, inner_weight, preferred_element_type=jnp.float32)
    hidden = lax.psum(partial_hidden.astype(jnp.bfloat16), "dp").astype(jnp.float32)
    active = activate(hidden, half_width)
    expert_out = jnp.dot(active, outer_weight, preferred_element_type=jnp.float32).astype(
        jnp.bfloat16
    )
    partial_act = lax.dot_general(
        scaled_cot, outer_weight, contract_cols, preferred_element_type=jnp.float32
    )
    act_grad = lax.psum(partial_act.astype(jnp.bfloat16), "dp").astype(jnp.float32)
    hidden_cot = activate_grad(hidden, act_grad, half_width)
    output_grad = lax.dot_general(
        active, scaled_cot, contract_rows, preferred_element_type=jnp.float32
    ).astype(jnp.bfloat16)
    hidden_grad = lax.dot_general(
        expert_rows, hidden_cot, contract_rows, preferred_element_type=jnp.float32
    ).astype(jnp.bfloat16)
    row_grad = lax.dot_general(
        hidden_cot, inner_weight, contract_cols, preferred_element_type=jnp.float32
    ).astype(jnp.bfloat16)
    returned = (
        lax.all_to_all(
            expert_out.reshape(send_shape), "expert", split_axis=0, concat_axis=0, tiled=True
        ),
        lax.all_to_all(
            row_grad.reshape(send_shape), "expert", split_axis=0, concat_axis=0, tiled=True
        ),
    )
    back_out = returned[0]
    back_grad = returned[1]
    back_out = back_out.reshape(row_total, column_width)
    back_grad = back_grad.reshape(row_total, column_width)
    weighted = placed * gate_slot[:, None]
    mixed = lax.dot_general(
        weighted,
        back_out.astype(jnp.float32),
        contract_rows,
        precision=lax.Precision.HIGHEST,
        preferred_element_type=jnp.float32,
    ).astype(jnp.bfloat16)
    token_grad = lax.dot_general(
        placed_half, back_grad, contract_rows, preferred_element_type=jnp.float32
    ).astype(jnp.bfloat16)
    return (mixed, token_grad, hidden_grad[None], output_grad[None])


def solution(mesh):
    return jax.shard_map(
        body,
        mesh=mesh,
        in_specs=(
            P("expert", "dp"),
            P("expert", "dp"),
            P("expert", None),
            P("expert", None),
            P("expert", "dp", None),
            P("expert", None, "dp"),
        ),
        out_specs=(
            P("expert", "dp"),
            P("expert", "dp"),
            P("expert", "dp", None),
            P("expert", None, "dp"),
        ),
        check_vma=False,
    )
```

profile of v0, /device:TPU:1, one launch (start us, length us, event | category | flops | bytes accessed | tf_op | source)
XLA Modules:
  0.0 334.4 jit_solution(6971142851061227383)
XLA Ops:
  7.2 1.0 copy.26
  8.2 0.1 eq.42
  8.3 0.1 eq.38
  8.4 9.1 %reduce-window.6 = s32[32,16,128]{2,1,0:T(8,128)S(1)} reduce-window(s32[32,16,128]{2,1,0:T(8,128)S(1)} %fusion.32, s32[]{:T(128)} %constant.6.clone.1), window={size=1x1x128 pad=0_0x0_0x127_0}, to_apply=%region_0.0 | reduce-window | flops 8323072 | bytes 524292 | tf_op jit(solution)/shard_map/reduce-window
  17.5 0.1 slice.18
  17.7 0.2 copy.31
  17.9 0.2 reduce-window.9
  18.1 0.1 broadcast_add_fusion
  18.2 0.1 fusion.29
  18.5 1.9 fusion
  20.5 1.3 select_reduce_fusion
  21.7 1.4 multiply_convert_fusion.1
  23.1 10.2 %all-to-all-start.2 = ((bf16[32,16,896]{2,1,0:T(8,128)(2,1)}), bf16[32,16,896]{2,1,0:T(8,128)(2,1)S(1)}, u32[]{:S(2)}, u32[]{:S(2)}) async-start(bf16[32,16,896]{2,1,0:T(8,128)(2,1)} %bitcast.65), calls=%async_computation.2 | async-start | bytes 1835008 | tf_op jit(solution)/shard_map/all_to_all | solution.py:69
  33.3 1.4 convolution_convert_fusion
  34.7 22.7 %all-to-all-done.2 = bf16[32,16,896]{2,1,0:T(8,128)(2,1)S(1)} async-done(((bf16[32,16,896]{2,1,0:T(8,128)(2,1)}), bf16[32,16,896]{2,1,0:T(8,128)(2,1)S(1)}, u32[]{:S(2)}, u32[]{:S(2)}) %all-to-all-start.2) | async-done | bytes 917536 | tf_op jit(solution)/shard_map/all_to_all | solution.py:69
  57.3 5.0 %all-to-all-start = ((bf16[32,16,896]{2,1,0:T(8,128)(2,1)}), bf16[32,16,896]{2,1,0:T(8,128)(2,1)}, u32[]{:S(2)}, u32[]{:S(2)}) async-start(bf16[32,16,896]{2,1,0:T(8,128)(2,1)} %bitcast.3), calls=%async_computation | async-start | bytes 1835008 | tf_op jit(solution)/shard_map/all_to_all | solution.py:68
  62.4 2.3 fusion.17
  64.7 21.8 %all-to-all-done = bf16[32,16,896]{2,1,0:T(8,128)(2,1)} async-done(((bf16[32,16,896]{2,1,0:T(8,128)(2,1)}), bf16[32,16,896]{2,1,0:T(8,128)(2,1)}, u32[]{:S(2)}, u32[]{:S(2)}) %all-to-all-start) | async-done | bytes 917536 | tf_op jit(solution)/shard_map/all_to_all | solution.py:68
  86.4 6.0 %fusion.5 = bf16[512,2048]{1,0:T(8,128)(2,1)} fusion(bf16[512,896]{1,0:T(8,128)(2,1)} %bitcast.4, bf16[1,896,2048]{2,1,0:T(8,128)(2,1)} %param.10), kind=kOutput, calls=%fused_computation.8 | convolution fusion | flops 1880096768 | bytes 6684672 | tf_op jit(solution)/shard_map/dot_general | solution.py:73
  92.4 160.4 %all-reduce.3.cloned.1.call-done = (bf16[512,2048]{1,0:T(8,128)(2,1)}, bf16[512,1024]{1,0:T(8,128)(2,1)}) async-done(((bf16[512,2048]{1,0:T(8,128)(2,1)}, bf16[512,1024]{1,0:T(8,128)(2,1)}), (bf16[512,2048]{1,0:T(8,128)(2,1)}, bf16[512,1024]{1,0:T(8,128)(2,1)})) %all-reduce.3.cloned.1.call-update) | async-done | bytes 3145744 | tf_op jit(solution)/shard_map/psum | solution.py:74
  252.9 2.2 convert_element_type.60
  255.1 2.3 fusion.10
  257.3 3.3 fusion.23
  260.6 10.7 %all-to-all-start.3 = ((bf16[32,16,896]{2,1,0:T(8,128)(2,1)}), bf16[32,16,896]{2,1,0:T(8,128)(2,1)}, u32[]{:S(2)}, u32[]{:S(2)}) async-start(bf16[32,16,896]{2,1,0:T(8,128)(2,1)} %bitcast.64), calls=%async_computation.3 | async-start | bytes 1835008 | tf_op jit(solution)/shard_map/all_to_all | solution.py:97
  271.3 3.4 %fusion.20 = bf16[512,896]{1,0:T(8,128)(2,1)} fusion(bf16[512,1024]{1,0:T(8,128)(2,1)} %get-tuple-element.8, bf16[1,1024,896]{2,1,0:T(8,128)(2,1)S(1)} %copy-done), kind=kOutput, calls=%fused_computation.26 | convolution fusion | flops 939982848 | bytes 3801088 | tf_op jit(solution)/shard_map/dot_general | solution.py:76
  274.7 20.7 %all-to-all-done.3 = bf16[32,16,896]{2,1,0:T(8,128)(2,1)} async-done(((bf16[32,16,896]{2,1,0:T(8,128)(2,1)}), bf16[32,16,896]{2,1,0:T(8,128)(2,1)}, u32[]{:S(2)}, u32[]{:S(2)}) %all-to-all-start.3) | async-done | bytes 917536 | tf_op jit(solution)/shard_map/all_to_all | solution.py:97
  295.4 5.0 %all-to-all-start.1 = ((bf16[32,16,896]{2,1,0:T(8,128)(2,1)}), bf16[32,16,896]{2,1,0:T(8,128)(2,1)}, u32[]{:S(2)}, u32[]{:S(2)}) async-start(bf16[32,16,896]{2,1,0:T(8,128)(2,1)} %bitcast.63), calls=%async_computation.1 | async-start | bytes 1835008 | tf_op jit(solution)/shard_map/all_to_all | solution.py:94
  300.4 4.1 %convert_bitcast_fusion.1 = bf16[1,1024,896]{2,1,0:T(8,128)(2,1)} fusion(bf16[512,1024]{1,0:T(8,128)(2,1)} %get-tuple-element.8, bf16[512,896]{1,0:T(8,128)(2,1)} %bitcast.62), kind=kOutput, calls=%fused_computation.23 | convolution fusion | flops 940441600 | bytes 3801088 | tf_op jit(solution)/shard_map/dot_general | solution.py:84
  304.5 5.1 %convert_bitcast_fusion = bf16[1,896,2048]{2,1,0:T(8,128)(2,1)} fusion(bf16[512,896]{1,0:T(8,128)(2,1)} %bitcast.4, bf16[512,1024]{1,0:T(8,128)(2,1)S(1)} %copy-done.2, bf16[512,1024]{1,0:T(8,128)(2,1)S(1)} %get-tuple-element.6), kind=kOutput, calls=%fused_computation.7 | convolution fusion | flops 1885077504 | bytes 6684672 | tf_op jit(solution)/shard_map/dot_general | solution.py:87
  309.6 2.4 convolution_convert_fusion.1
  312.1 12.5 %all-to-all-done.1 = bf16[32,16,896]{2,1,0:T(8,128)(2,1)} async-done(((bf16[32,16,896]{2,1,0:T(8,128)(2,1)}), bf16[32,16,896]{2,1,0:T(8,128)(2,1)}, u32[]{:S(2)}, u32[]{:S(2)}) %all-to-all-start.1) | async-done | bytes 917536 | tf_op jit(solution)/shard_map/all_to_all | solution.py:94
  324.5 3.1 convolution_convert_fusion.2
  (26 shorter events, 0.3 us)
Async XLA Ops:
  7.2 55.2 %copy-start = (bf16[1,1024,896]{2,1,0:T(8,128)(2,1)S(1)}, bf16[1,1024,896]{2,1,0:T(8,128)(2,1)}, u32[]{:S(2)}) copy-start(bf16[1,1024,896]{2,1,0:T(8,128)(2,1)} %param.11) | copy-start | bytes 5505028
  7.2 11.3 %copy-start.6 = (s32[256,8]{0,1:T(8,128)S(1)}, s32[256,8]{0,1:T(8,128)}, u32[]{:S(2)}) copy-start(s32[256,8]{0,1:T(8,128)} %param.8) | copy-start | bytes 24580
  7.2 13.3 %copy-start.7 = (f32[256,8]{0,1:T(8,128)S(1)}, f32[256,8]{0,1:T(8,128)}, u32[]{:S(2)}) copy-start(f32[256,8]{0,1:T(8,128)} %param.9) | copy-start | bytes 24580
  7.2 14.5 %copy-start.9 = (bf16[256,896]{1,0:T(8,128)(2,1)S(1)}, bf16[256,896]{1,0:T(8,128)(2,1)}, u32[]{:S(2)}) copy-start(bf16[256,896]{1,0:T(8,128)(2,1)} %param.7) | copy-start | bytes 1376260
  18.2 15.1 %copy-start.5 = (bf16[256,896]{1,0:T(8,128)(2,1)S(1)}, bf16[256,896]{1,0:T(8,128)(2,1)}, u32[]{:S(2)}) copy-start(bf16[256,896]{1,0:T(8,128)(2,1)} %param.6) | copy-start | bytes 1376260
  23.1 34.2 %all-to-all-start.2 = ((bf16[32,16,896]{2,1,0:T(8,128)(2,1)}), bf16[32,16,896]{2,1,0:T(8,128)(2,1)S(1)}, u32[]{:S(2)}, u32[]{:S(2)}) async-start(bf16[32,16,896]{2,1,0:T(8,128)(2,1)} %bitcast.65), calls=%async_computation.2 | async-start | bytes 1835008 | tf_op jit(solution)/shard_map/all_to_all | solution.py:69
  57.3 7.3 %copy-start.4 = (bf16[32,16,896]{2,1,0:T(8,128)(2,1)}, bf16[32,16,896]{2,1,0:T(8,128)(2,1)S(1)}, u32[]{:S(2)}) copy-start(bf16[32,16,896]{2,1,0:T(8,128)(2,1)S(1)} %all-to-all-done.2) | copy-start | bytes 2752516
  57.3 29.1 %all-to-all-start = ((bf16[32,16,896]{2,1,0:T(8,128)(2,1)}), bf16[32,16,896]{2,1,0:T(8,128)(2,1)}, u32[]{:S(2)}, u32[]{:S(2)}) async-start(bf16[32,16,896]{2,1,0:T(8,128)(2,1)} %bitcast.3), calls=%async_computation | async-start | bytes 1835008 | tf_op jit(solution)/shard_map/all_to_all | solution.py:68
  62.3 190.5 %all-reduce.3.cloned.1.call-start = ((), (), s32[]{:S(2)}) async-start(), calls=%async_computation.4 | async-start | bytes 6291456 | tf_op jit(solution)/shard_map/psum | solution.py:74
  252.9 2.2 copy-start.3
  255.1 2.3 copy-start.8
  257.3 3.3 copy-start.1
  260.6 34.8 %all-to-all-start.3 = ((bf16[32,16,896]{2,1,0:T(8,128)(2,1)}), bf16[32,16,896]{2,1,0:T(8,128)(2,1)}, u32[]{:S(2)}, u32[]{:S(2)}) async-start(bf16[32,16,896]{2,1,0:T(8,128)(2,1)} %bitcast.64), calls=%async_computation.3 | async-start | bytes 1835008 | tf_op jit(solution)/shard_map/all_to_all | solution.py:97
  295.4 29.1 %all-to-all-start.1 = ((bf16[32,16,896]{2,1,0:T(8,128)(2,1)}), bf16[32,16,896]{2,1,0:T(8,128)(2,1)}, u32[]{:S(2)}, u32[]{:S(2)}) async-start(bf16[32,16,896]{2,1,0:T(8,128)(2,1)} %bitcast.63), calls=%async_computation.1 | async-start | bytes 1835008 | tf_op jit(solution)/shard_map/all_to_all | solution.py:94
  300.4 4.1 %copy-start.2 = (bf16[512,1024]{1,0:T(8,128)(2,1)S(1)}, bf16[512,1024]{1,0:T(8,128)(2,1)}, u32[]{:S(2)}) copy-start(bf16[512,1024]{1,0:T(8,128)(2,1)} %copy-done.1) | copy-start | bytes 3145732
Sparse Core Ops, SparseCore 0:
  92.6 160.2 all-reduce.2
where the time goes:
time: 335 us; the launch traced here: 334 us
  waiting for transfers between devices  238 us (71%)
  matrix products  32.4 us (10%)
  starting transfers between devices  30.9 us (9%)
  other arithmetic  17.2 us (5%)
  between operations  14.2 us (4%)
    psum x1, waiting for transfers between devices, body(): lax.psum(partial_hidden.astype(jnp.bfloat16), 'dp').astype(jnp.float32)  160 us
    all_to_all x1, waiting for transfers between devices, body(): lax.all_to_all(cot_rows, 'expert', split_axis=0, concat_axis=0, tiled=True)  22.7 us
    all_to_all x1, waiting for transfers between devices, body(): lax.all_to_all(token_rows, 'expert', split_axis=0, concat_axis=0, tiled=T...  21.8 us
    all_to_all x1, waiting for transfers between devices, body(): lax.all_to_all(row_grad.reshape(send_shape), 'expert', split_axis=0, conc...  20.7 us
    all_to_all x1, waiting for transfers between devices, body(): lax.all_to_all(expert_out.reshape(send_shape), 'expert', split_axis=0, co...  12.5 us
    another operation x4, other arithmetic  11.7 us
    all_to_all x1, starting transfers between devices, body(): lax.all_to_all(row_grad.reshape(send_shape), 'expert', split_axis=0, conc...  10.7 us
    all_to_all x1, starting transfers between devices, body(): lax.all_to_all(cot_rows, 'expert', split_axis=0, concat_axis=0, tiled=True)  10.2 us
  transfers between devices with their start and end apart: 5, of which 5 were waited for; matrix products, arithmetic and copies ran while one was open for 6% of the time, Pallas kernels for 0%

commit v1 on v0

v1 whole, which is shorter than its diff:
```python
import functools

import jax
import jax.numpy as jnp
from jax import lax
from jax.experimental import pallas as pl
from jax.experimental.pallas import tpu as pltpu
from jax.sharding import PartitionSpec as P

MESH = pl.DeviceIdType.MESH
F32 = jnp.float32
BF16 = jnp.bfloat16
SLOTS = 16
EXPERTS = 32
CHUNKS = 8
PER = EXPERTS // CHUNKS
SPLIT = CHUNKS // 4
ROWS = PER * SLOTS
NX = 4
QUART = ROWS // NX
VMEM_LIMIT = 40 * 2**20
LAST = (((1,), (1,)), ((), ()))
FIRST = (((0,), (0,)), ((), ()))

SCHEDULE = ('D0', 'D1', 'D2', 'd0', 'D3', 'p0', 't0', 'd1', 'D4', 'p1', 'r0', 'd2', 'D5', 'p2', 'r1', 'z0', 'd3', 'D6', 'p3', 'r2', 'z1', 'g0', 'd4', 'D7', 'p4', 'r3', 'z2', 'g1', 'd5', 'p5', 'r4', 'z3', 'g2', 'd6', 'p6', 'r5', 'z4', 'g3', 'd7', 'p7', 'r6', 'z5', 'g4', 'r7', 'z6', 'g5', 'z7', 'g6', 'g7', 'o0', 'h0', 'c0', 'c1', 'c2', 'c3', 'c4', 'c5', 'c6', 'c7')


def kernel(
    routing_hbm,
    gate_hbm,
    tok_hbm,
    cot_hbm,
    w1_hbm,
    w2_hbm,
    mixed_ref,
    tgrad_ref,
    hgrad_ref,
    ograd_ref,
    routing_ref,
    gate_ref,
    tok_ref,
    cot_ref,
    w1,
    w2,
    place,
    whi,
    wlo,
    send,
    recv,
    part,
    xrecv,
    zsend,
    zrecv,
    act,
    rsend,
    rrecv,
    rows_t,
    place_t,
    whi_t,
    wlo_t,
    mixed_sum,
    grad_sum,
    w_sem,
    d_send,
    d_recv,
    x_send,
    x_recv,
    z_send,
    z_recv,
    g_send,
    g_recv,
    r_send,
    r_recv,
):
    pairs = (
        (routing_hbm, routing_ref),
        (gate_hbm, gate_ref),
        (tok_hbm, tok_ref),
        (cot_hbm, cot_ref),
        (w1_hbm, w1),
        (w2_hbm, w2),
    )
    loads = [pltpu.make_async_copy(*pair, w_sem.at[i]) for i, pair in enumerate(pairs)]
    load1, load2 = loads[4:]
    for load in loads[:4]:
        load.start()
    dp = lax.axis_index("dp")
    me = lax.axis_index("expert")
    zh, x = dp // NX, dp % NX
    zl, y, core = me // 8, (me // 2) % 4, me % 2
    half = w2.shape[0]
    toks = tok_ref.shape[0]
    width = tok_ref.shape[1]
    z_peer = (1 - zh) * NX + x

    def x_peer(i):
        return zh * NX + (x + i) % NX

    def target(c, k):
        if SPLIT == 2:
            return k * 8 + ((y + 4 - c // 2) % 4) * 2 + (core + c) % 2
        return (k // 2) * 8 + ((y + 4 - c) % 4) * 2 + k % 2

    def origin(c, k):
        if SPLIT == 2:
            return k * 8 + ((y + c // 2) % 4) * 2 + (core + c) % 2
        return (k // 2) * 8 + ((y + c) % 4) * 2 + k % 2

    mine = zl if SPLIT == 2 else zl * 2 + core

    barrier = pltpu.get_barrier_semaphore()

    def greet(j, carry):
        pl.semaphore_signal(
            barrier, inc=1, device_id=(dp, (me + j) % EXPERTS), device_id_type=MESH
        )
        return carry

    lax.fori_loop(1, EXPERTS, greet, 0)
    for i in range(1, NX):
        pl.semaphore_signal(barrier, inc=1, device_id=(x_peer(i), me), device_id_type=MESH)
    pl.semaphore_signal(barrier, inc=1, device_id=(z_peer, me), device_id_type=MESH)

    load1.start()
    load2.start()
    loads[0].wait()
    loads[1].wait()

    ids = lax.broadcasted_iota(jnp.int32, (EXPERTS, toks), 0)
    member = jnp.zeros((EXPERTS, toks), F32)
    gates = jnp.zeros((EXPERTS, toks), F32)
    for k in range(routing_ref.shape[0]):
        hit = routing_ref[k : k + 1, :] == ids
        member = jnp.where(hit, 1.0, member)
        gates = jnp.where(hit, gate_ref[k : k + 1, :], gates)
    earlier = lax.broadcasted_iota(jnp.int32, (toks, toks), 0) < lax.broadcasted_iota(
        jnp.int32, (toks, toks), 1
    )
    earlier = jnp.where(earlier, 1.0, 0.0).astype(BF16)
    rank = jnp.dot(member.astype(BF16), earlier, preferred_element_type=F32)
    rank = jnp.where(member > 0.0, rank, -1.0).astype(BF16)
    slots = EXPERTS * SLOTS
    order = lax.broadcasted_iota(jnp.int32, (slots, EXPERTS), 0) >> 4
    spread = target(order // PER, order % PER) == lax.broadcasted_iota(
        jnp.int32, (slots, EXPERTS), 1
    )
    spread = jnp.where(spread, 1.0, 0.0).astype(BF16)
    within = lax.broadcasted_iota(jnp.int32, (slots, toks), 0) & (SLOTS - 1)
    hits = jnp.dot(spread, rank, preferred_element_type=F32) == within.astype(F32)
    high = gates.astype(BF16)
    low = (gates - high.astype(F32)).astype(BF16)
    place[...] = jnp.where(hits, 1.0, 0.0).astype(BF16)
    whi[...] = jnp.where(
        hits, jnp.dot(spread, high, preferred_element_type=F32), 0.0
    ).astype(BF16)
    wlo[...] = jnp.where(
        hits, jnp.dot(spread, low, preferred_element_type=F32), 0.0
    ).astype(BF16)

    def pick(c):
        at = pl.ds(c * ROWS, ROWS)
        rows = jnp.dot(place[at, :], tok_ref[...], preferred_element_type=F32)
        send[c, :, 0] = rows.astype(BF16).reshape(PER, SLOTS, width)
        rows = jnp.dot(whi[at, :], cot_ref[...], preferred_element_type=F32)
        rows += jnp.dot(wlo[at, :], cot_ref[...], preferred_element_type=F32)
        send[c, :, 1] = rows.astype(BF16).reshape(PER, SLOTS, width)

    def dispatch_copy(c, j):
        k = (mine + j) % PER
        to = target(c, k)
        return pltpu.make_async_remote_copy(
            src_ref=send.at[c, k],
            dst_ref=recv.at[c, mine],
            send_sem=d_send.at[c, j],
            recv_sem=d_recv.at[c, mine],
            device_id=(dp, to),
            device_id_type=MESH,
        )

    def own_dispatch():
        return pltpu.make_async_copy(
            send.at[0, mine], recv.at[0, mine], d_recv.at[0, mine]
        )

    def return_copy(c, j):
        k = (mine + j) % PER
        to = origin(c, k)
        return pltpu.make_async_remote_copy(
            src_ref=rsend.at[c, k],
            dst_ref=rrecv.at[c, mine],
            send_sem=r_send.at[c, j],
            recv_sem=r_recv.at[c, mine],
            device_id=(dp, to),
            device_id_type=MESH,
        )

    def own_return():
        return pltpu.make_async_copy(
            rsend.at[0, mine], rrecv.at[0, mine], r_recv.at[0, mine]
        )

    def scatter_copy(c, i):
        to = (x + i) % NX
        return pltpu.make_async_remote_copy(
            src_ref=part.at[c, pl.ds(to * QUART, QUART)],
            dst_ref=xrecv.at[c, i - 1],
            send_sem=x_send.at[c, i - 1],
            recv_sem=x_recv.at[c, i - 1],
            device_id=(x_peer(i), me),
            device_id_type=MESH,
        )

    def exchange_copy(c):
        return pltpu.make_async_remote_copy(
            src_ref=zsend.at[c],
            dst_ref=zrecv.at[c],
            send_sem=z_send.at[c],
            recv_sem=z_recv.at[c],
            device_id=(z_peer, me),
            device_id_type=MESH,
        )

    def gather_copy(c, i, owner):
        block = pl.ds(owner * QUART, QUART)
        return pltpu.make_async_remote_copy(
            src_ref=act.at[c, block],
            dst_ref=act.at[c, block],
            send_sem=g_send.at[c, i - 1],
            recv_sem=g_recv.at[c, i - 1],
            device_id=(x_peer(i), me),
            device_id_type=MESH,
        )

    def start_dispatch(c):
        if c > 0:
            pick(c)
        else:
            own_dispatch().start()

        def one(j, carry):
            dispatch_copy(c, j).start()
            return carry

        lax.fori_loop(1 if c == 0 else 0, PER, one, 0)

    def wait_dispatch(c):
        def one(k, carry):
            pltpu.make_async_copy(recv.at[c, k], recv.at[c, k], d_recv.at[c, k]).wait()
            return carry

        lax.fori_loop(0, PER, one, 0)

    def products(c):
        if c == 0:
            load1.wait()
            load2.wait()
        tok_rows = recv[c, :, 0].reshape(ROWS, width)
        cot_rows = recv[c, :, 1].reshape(ROWS, width)
        tile = 512

        def hidden_tile(n, carry):
            at = pl.ds(pl.multiple_of(n * tile, tile), tile)
            part[c, :, at] = jnp.dot(
                recv[c, :, 0].reshape(ROWS, width), w1[:, at], preferred_element_type=F32
            ).astype(BF16)
            return carry

        lax.fori_loop(0, 2 * half // tile, hidden_tile, 0)

        def act_tile(n, carry):
            at = pl.ds(pl.multiple_of(n * tile, tile), tile)
            to = pl.ds(pl.multiple_of(2 * half + n * tile, tile), tile)
            part[c, :, to] = lax.dot_general(
                recv[c, :, 1].reshape(ROWS, width), w2[at, :], LAST, preferred_element_type=F32
            ).astype(BF16)
            return carry

        lax.fori_loop(0, half // tile, act_tile, 0)
        for i in range(1, NX):
            scatter_copy(c, i).start()

    def reduce_x(c):
        for i in range(1, NX):
            scatter_copy(c, i).wait_recv()
        own = part[c, pl.ds(pl.multiple_of(x * QUART, QUART), QUART)].astype(F32)
        total = own + xrecv[c, 0].astype(F32)
        total += xrecv[c, 1].astype(F32)
        total += xrecv[c, 2].astype(F32)
        zsend[c] = total.astype(BF16)
        exchange_copy(c).start()

    def activate(c):
        exchange_copy(c).wait_recv()
        total = zsend[c].astype(F32) + zrecv[c].astype(F32)
        gate = total[:, :half]
        up = total[:, half : 2 * half]
        grad = total[:, 2 * half :]
        sig = jax.nn.sigmoid(gate)
        silu = gate * sig
        block = pl.ds(pl.multiple_of(x * QUART, QUART), QUART)
        act[c, block, 0:half] = (silu * up).astype(BF16)
        act[c, block, half : 2 * half] = (
            grad * up * sig * (1.0 + gate * (1.0 - sig))
        ).astype(BF16)
        act[c, block, 2 * half :] = (grad * silu).astype(BF16)
        for i in range(1, NX):
            gather_copy(c, i, x).start()

    def results(c):
        for i in range(1, NX):
            gather_copy(c, i, (x + NX - i) % NX).wait_recv()
        out = jnp.dot(act[c, :, 0:half], w2[...], preferred_element_type=F32)
        rsend[c, :, 0] = out.astype(BF16).reshape(PER, SLOTS, width)
        out = lax.dot_general(
            act[c, :, half:], w1[...], LAST, preferred_element_type=F32
        )
        rsend[c, :, 1] = out.astype(BF16).reshape(PER, SLOTS, width)
        if c == 0:
            own_return().start()

        def one(j, carry):
            return_copy(c, j).start()
            return carry

        lax.fori_loop(1 if c == 0 else 0, PER, one, 0)

    def transposes():
        place_t[...] = place[...].T
        whi_t[...] = whi[...].T
        wlo_t[...] = wlo[...].T

    def combine(c):
        def arrived(k, carry):
            pltpu.make_async_copy(rrecv.at[c, k], rrecv.at[c, k], r_recv.at[c, k]).wait()
            return carry

        lax.fori_loop(0, PER, arrived, 0)
        at = pl.ds(c * ROWS, ROWS)
        back = rrecv[c, :, 0].reshape(ROWS, width)
        mixed = jnp.dot(whi_t[:, at], back, preferred_element_type=F32)
        mixed += jnp.dot(wlo_t[:, at], back, preferred_element_type=F32)
        back = rrecv[c, :, 1].reshape(ROWS, width)
        grads = jnp.dot(place_t[:, at], back, preferred_element_type=F32)
        if c > 0:
            mixed += mixed_sum[...]
            grads += grad_sum[...]
        if c < CHUNKS - 1:
            mixed_sum[...] = mixed
            grad_sum[...] = grads
        else:
            mixed_ref[...] = mixed.astype(BF16)
            tgrad_ref[...] = grads.astype(BF16)

    loads[2].wait()
    loads[3].wait()
    pick(0)
    pl.semaphore_wait(barrier, EXPERTS - 1 + NX)

    run = {
        "D": start_dispatch,
        "d": wait_dispatch,
        "p": products,
        "r": reduce_x,
        "z": activate,
        "g": results,
    }
    def output_gradient(_):
        tile = 256

        def one(n, carry):
            at = pl.ds(pl.multiple_of(n * tile, tile), tile)
            ograd_ref[at, :] = lax.dot_general(
                act[:, :, at].reshape(slots, tile),
                recv[:, :, 1].reshape(slots, width),
                FIRST,
                preferred_element_type=F32,
            ).astype(BF16)
            return carry

        lax.fori_loop(0, half // tile, one, 0)

    def hidden_gradient(_):
        tile = 256
        rows_t[...] = recv[:, :, 0].reshape(slots, width).T

        def one(n, carry):
            at = pl.ds(pl.multiple_of(n * tile, tile), tile)
            cots = act[:, :, pl.ds(pl.multiple_of(half + n * tile, tile), tile)]
            hgrad_ref[:, at] = jnp.dot(
                rows_t[...], cots.reshape(slots, tile), preferred_element_type=F32
            ).astype(BF16)
            return carry

        lax.fori_loop(0, 2 * half // tile, one, 0)

    run["t"] = lambda _: transposes()
    run["o"] = output_gradient
    run["h"] = hidden_gradient
    run["c"] = combine
    for step in SCHEDULE:
        run[step[0]](int(step[1]))

    for c in range(CHUNKS):

        def left(j, carry):
            dispatch_copy(c, j).wait_send()
            return_copy(c, j).wait_send()
            return carry

        lax.fori_loop(1 if c == 0 else 0, PER, left, 0)
        for i in range(1, NX):
            scatter_copy(c, i).wait_send()
            gather_copy(c, i, x).wait_send()
        exchange_copy(c).wait_send()


def store_kernel(*refs):
    ins, outs, sem = refs[:4], refs[4:8], refs[8]
    copies = [
        pltpu.make_async_copy(ins[i], outs[i], sem.at[i]) for i in range(4)
    ]
    for copy in copies:
        copy.start()
    for copy in copies:
        copy.wait()


def body(tokens, cotangent, routing, gate_values, hidden_weight, output_weight):
    toks, width = tokens.shape
    half = output_weight.shape[1]
    wide = 3 * half
    dma = pltpu.SemaphoreType.DMA
    vmem = pl.BlockSpec(memory_space=pltpu.VMEM)
    hbm = pl.BlockSpec(memory_space=pltpu.HBM)
    shapes = ((toks, width), (toks, width), (width, 2 * half), (half, width))
    slots = EXPERTS * SLOTS
    made = pl.pallas_call(
        kernel,
        name="moe_layer",
        out_shape=[pltpu.VMEM(shape, BF16) for shape in shapes],
        in_specs=[hbm] * 6,
        out_specs=[vmem] * 4,
        scratch_shapes=[
            pltpu.VMEM(routing.shape[::-1], jnp.int32),
            pltpu.VMEM(routing.shape[::-1], F32),
            pltpu.VMEM((toks, width), BF16),
            pltpu.VMEM((toks, width), BF16),
            pltpu.VMEM((width, 2 * half), BF16),
            pltpu.VMEM((half, width), BF16),
            pltpu.VMEM((slots, toks), BF16),
            pltpu.VMEM((slots, toks), BF16),
            pltpu.VMEM((slots, toks), BF16),
            pltpu.VMEM((CHUNKS, PER, 2, SLOTS, width), BF16),
            pltpu.VMEM((CHUNKS, PER, 2, SLOTS, width), BF16),
            pltpu.VMEM((CHUNKS, ROWS, wide), BF16),
            pltpu.VMEM((CHUNKS, NX - 1, QUART, wide), BF16),
            pltpu.VMEM((CHUNKS, QUART, wide), BF16),
            pltpu.VMEM((CHUNKS, QUART, wide), BF16),
            pltpu.VMEM((CHUNKS, ROWS, wide), BF16),
            pltpu.VMEM((CHUNKS, PER, 2, SLOTS, width), BF16),
            pltpu.VMEM((CHUNKS, PER, 2, SLOTS, width), BF16),
            pltpu.VMEM((width, slots), BF16),
            pltpu.VMEM((toks, slots), BF16),
            pltpu.VMEM((toks, slots), BF16),
            pltpu.VMEM((toks, slots), BF16),
            pltpu.VMEM((toks, width), F32),
            pltpu.VMEM((toks, width), F32),
            dma((6,)),
            dma((CHUNKS, PER)),
            dma((CHUNKS, PER)),
            dma((CHUNKS, NX - 1)),
            dma((CHUNKS, NX - 1)),
            dma((CHUNKS,)),
            dma((CHUNKS,)),
            dma((CHUNKS, NX - 1)),
            dma((CHUNKS, NX - 1)),
            dma((CHUNKS, PER)),
            dma((CHUNKS, PER)),
        ],
        compiler_params=pltpu.CompilerParams(
            collective_id=0, has_side_effects=True, vmem_limit_bytes=VMEM_LIMIT
        ),
    )(
        *[
            pltpu.with_memory_space_constraint(value, pltpu.HBM)
            for value in (
                routing.T,
                gate_values.T,
                tokens,
                cotangent,
                hidden_weight[0],
                output_weight[0],
            )
        ]
    )
    made = [pltpu.with_memory_space_constraint(value, pltpu.VMEM) for value in made]
    mixed, token_grad, hidden_grad, output_grad = pl.pallas_call(
        store_kernel,
        name="store",
        out_shape=[jax.ShapeDtypeStruct(shape, BF16) for shape in shapes],
        in_specs=[vmem] * 4,
        out_specs=[hbm] * 4,
        scratch_shapes=[dma((4,))],
        compiler_params=pltpu.CompilerParams(vmem_limit_bytes=2**20),
    )(*made)
    return mixed, token_grad, hidden_grad[None], output_grad[None]


def solution(mesh):
    return jax.shard_map(
        body,
        mesh=mesh,
        in_specs=(
            P("expert", "dp"),
            P("expert", "dp"),
            P("expert", None),
            P("expert", None),
            P("expert", "dp", None),
            P("expert", None, "dp"),
        ),
        out_specs=(
            P("expert", "dp"),
            P("expert", "dp"),
            P("expert", "dp", None),
            P("expert", None, "dp"),
        ),
        check_vma=False,
    )
```

time: 335 us -> 136 us (0.41)
  the two profiles are of different devices: /device:TPU:1 before, /device:TPU:97 now
where the time goes in v1:
time: 136 us
  Pallas kernels  135 us (99%)
    pallas_call x1, Pallas kernels, body(): pl.pallas_call(kernel, name='moe_layer', out_shape=[pltpu.VMEM(shape, BF1...  132 us
    pallas_call x1, Pallas kernels, body(): pl.pallas_call(store_kernel, name='store', out_shape=[jax.ShapeDtypeStruc...  2.78 us

profile of v1, /device:TPU:97, one launch (start us, length us, event | category | flops | bytes accessed | tf_op | source)
XLA Modules:
  0.0 135.5 jit_solution(13625614909317646181)
XLA Ops:
  0.6 132.0 %moe_layer.1 = (bf16[256,896]{1,0:T(8,128)(2,1)S(1)}, bf16[256,896]{1,0:T(8,128)(2,1)S(1)}, bf16[896,2048]{1,0:T(8,128)(2,1)S(1)}, bf16[1024,896]{1,0:T(8,128)(2,1)S(1)}) custom-call(s32[8,256]{1,0:T(8,128)} %bitcast.8, f32[8,256]{1,0:T(8,128)} %bitcast.9, bf16[256,896]{1,0:T(8,128)(2,1)} %tok_hbm.1, bf16[256,896]{1,0:T(8,128)(2,1)} %cot_hbm.1, ...), custom_call_target="tpu_custom_call" | custom-call | tf_op jit(solution)/shard_map/moe_layer/pallas_call | solution.py:437
  132.6 2.8 %store.1 = (bf16[256,896]{1,0:T(8,128)(2,1)}, bf16[256,896]{1,0:T(8,128)(2,1)}, bf16[896,2048]{1,0:T(8,128)(2,1)}, bf16[1024,896]{1,0:T(8,128)(2,1)}) custom-call(bf16[256,896]{1,0:T(8,128)(2,1)S(1)} %get-tuple-element.12.refs_0_, bf16[256,896]{1,0:T(8,128)(2,1)S(1)} %get-tuple-element.13.refs_1_, bf16[896,2048]{1,0:T(8,128)(2,1)S(1)} %get-tuple-element.14.refs_2_, ...), custom_call_target="tpu_custom_call" | custom-call | tf_op jit(solution)/shard_map/store/pallas_call | solution.py:497

commit v2 on v1

--- a/solution.py
+++ b/solution.py
@@ -19,10 +19,16 @@
 NX = 4
 QUART = ROWS // NX
 VMEM_LIMIT = 40 * 2**20
+STORES = 4
+XP = 1
+ZP = 3
+AP = 1
+DP = 2
+RP = 1
 LAST = (((1,), (1,)), ((), ()))
 FIRST = (((0,), (0,)), ((), ()))
 
-SCHEDULE = ('D0', 'D1', 'D2', 'd0', 'D3', 'p0', 't0', 'd1', 'D4', 'p1', 'r0', 'd2', 'D5', 'p2', 'r1', 'z0', 'd3', 'D6', 'p3', 'r2', 'z1', 'g0', 'd4', 'D7', 'p4', 'r3', 'z2', 'g1', 'd5', 'p5', 'r4', 'z3', 'g2', 'd6', 'p6', 'r5', 'z4', 'g3', 'd7', 'p7', 'r6', 'z5', 'g4', 'r7', 'z6', 'g5', 'z7', 'g6', 'g7', 'o0', 'h0', 'c0', 'c1', 'c2', 'c3', 'c4', 'c5', 'c6', 'c7')
+SCHEDULE = ('D0', 'D1', 'D2', 'D3', 'D4', 'D5', 'D6', 'D7', 'd0', 'p0', 't0', 'd1', 'p1', 'r0', 'd2', 'p2', 'r1', 'z0', 'd3', 'p3', 'r2', 'z1', 'g0', 'd4', 'p4', 'r3', 'z2', 'g1', 'd5', 'p5', 'r4', 'z3', 'g2', 'd6', 'p6', 'r5', 'z4', 'g3', 'd7', 'p7', 'r6', 'z5', 'g4', 'r7', 'z6', 'g5', 'z7', 'g6', 'g7', 'o0', 'h0', 'c0', 'c1', 'c2', 'c3', 'c4', 'c5', 'c6', 'c7')
 
 
 def kernel(
@@ -150,112 +156,139 @@
     high = gates.astype(BF16)
     low = (gates - high.astype(F32)).astype(BF16)
     place[...] = jnp.where(hits, 1.0, 0.0).astype(BF16)
-    whi[...] = jnp.where(
-        hits, jnp.dot(spread, high, preferred_element_type=F32), 0.0
-    ).astype(BF16)
-    wlo[...] = jnp.where(
-        hits, jnp.dot(spread, low, preferred_element_type=F32), 0.0
-    ).astype(BF16)
-
-    def pick(c):
+
+    def gate_tables():
+        whi[...] = jnp.where(
+            hits, jnp.dot(spread, high, preferred_element_type=F32), 0.0
+        ).astype(BF16)
+        wlo[...] = jnp.where(
+            hits, jnp.dot(spread, low, preferred_element_type=F32), 0.0
+        ).astype(BF16)
+
+    def pick_tokens(c):
         at = pl.ds(c * ROWS, ROWS)
         rows = jnp.dot(place[at, :], tok_ref[...], preferred_element_type=F32)
         send[c, :, 0] = rows.astype(BF16).reshape(PER, SLOTS, width)
+
+    def pick_cotangents(c):
+        at = pl.ds(c * ROWS, ROWS)
         rows = jnp.dot(whi[at, :], cot_ref[...], preferred_element_type=F32)
         rows += jnp.dot(wlo[at, :], cot_ref[...], preferred_element_type=F32)
         send[c, :, 1] = rows.astype(BF16).reshape(PER, SLOTS, width)
 
-    def dispatch_copy(c, j):
+    def rows_part(ref, q, pieces):
+        return ref if pieces == 1 else ref.at[q]
+
+    def columns(q, pieces):
+        return pl.ds(q * (3 * half // pieces), 3 * half // pieces)
+
+    def dispatch_copy(c, j, q):
         k = (mine + j) % PER
         to = target(c, k)
         return pltpu.make_async_remote_copy(
-            src_ref=send.at[c, k],
-            dst_ref=recv.at[c, mine],
-            send_sem=d_send.at[c, j],
-            recv_sem=d_recv.at[c, mine],
+            src_ref=rows_part(send.at[c, k], q, DP),
+            dst_ref=rows_part(recv.at[c, mine], q, DP),
+            send_sem=d_send.at[c, q, j],
+            recv_sem=d_recv.at[c, q, mine],
             device_id=(dp, to),
             device_id_type=MESH,
         )
 
-    def own_dispatch():
+    def own_dispatch(q):
         return pltpu.make_async_copy(
-            send.at[0, mine], recv.at[0, mine], d_recv.at[0, mine]
-        )
-
-    def return_copy(c, j):
+            rows_part(send.at[0, mine], q, DP),
+            rows_part(recv.at[0, mine], q, DP),
+            d_recv.at[0, q, mine],
+        )
+
+    def return_copy(c, j, q):
         k = (mine + j) % PER
         to = origin(c, k)
         return pltpu.make_async_remote_copy(
-            src_ref=rsend.at[c, k],
-            dst_ref=rrecv.at[c, mine],
-            send_sem=r_send.at[c, j],
-            recv_sem=r_recv.at[c, mine],
+            src_ref=rows_part(rsend.at[c, k], q, RP),
+            dst_ref=rows_part(rrecv.at[c, mine], q, RP),
+            send_sem=r_send.at[c, q, j],
+            recv_sem=r_recv.at[c, q, mine],
             device_id=(dp, to),
             device_id_type=MESH,
         )
 
-    def own_return():
+    def own_return(q):
         return pltpu.make_async_copy(
-            rsend.at[0, mine], rrecv.at[0, mine], r_recv.at[0, mine]
-        )
-
-    def scatter_copy(c, i):
+            rows_part(rsend.at[0, mine], q, RP),
+            rows_part(rrecv.at[0, mine], q, RP),
+            r_recv.at[0, q, mine],
+        )
+
+    def scatter_copy(c, i, q):
         to = (x + i) % NX
         return pltpu.make_async_remote_copy(
-            src_ref=part.at[c, pl.ds(to * QUART, QUART)],
-            dst_ref=xrecv.at[c, i - 1],
-            send_sem=x_send.at[c, i - 1],
-            recv_sem=x_recv.at[c, i - 1],
+            src_ref=part.at[c, pl.ds(to * QUART, QUART), columns(q, XP)],
+            dst_ref=xrecv.at[c, i - 1, :, columns(q, XP)],
+            send_sem=x_send.at[c, i - 1, q],
+            recv_sem=x_recv.at[c, i - 1, q],
             device_id=(x_peer(i), me),
             device_id_type=MESH,
         )
 
-    def exchange_copy(c):
+    def exchange_copy(c, q):
         return pltpu.make_async_remote_copy(
-            src_ref=zsend.at[c],
-            dst_ref=zrecv.at[c],
-            send_sem=z_send.at[c],
-            recv_sem=z_recv.at[c],
+            src_ref=zsend.at[c, :, columns(q, ZP)],
+            dst_ref=zrecv.at[c, :, columns(q, ZP)],
+            send_sem=z_send.at[c, q],
+            recv_sem=z_recv.at[c, q],
             device_id=(z_peer, me),
             device_id_type=MESH,
         )
 
-    def gather_copy(c, i, owner):
+    def gather_copy(c, i, owner, q):
         block = pl.ds(owner * QUART, QUART)
         return pltpu.make_async_remote_copy(
-            src_ref=act.at[c, block],
-            dst_ref=act.at[c, block],
-            send_sem=g_send.at[c, i - 1],
-            recv_sem=g_recv.at[c, i - 1],
+            src_ref=act.at[c, block, columns(q, AP)],
+            dst_ref=act.at[c, block, columns(q, AP)],
+            send_sem=g_send.at[c, i - 1, q],
+            recv_sem=g_recv.at[c, i - 1, q],
             device_id=(x_peer(i), me),
             device_id_type=MESH,
         )
 
+    def send_rows(c, q):
+        if c == 0:
+            own_dispatch(q).start()
+
+        def one(j, carry):
+            dispatch_copy(c, j, q).start()
+            return carry
+
+        lax.fori_loop(1 if c == 0 else 0, PER, one, 0)
+
     def start_dispatch(c):
         if c > 0:
-            pick(c)
-        else:
-            own_dispatch().start()
-
-        def one(j, carry):
-            dispatch_copy(c, j).start()
-            return carry
-
-        lax.fori_loop(1 if c == 0 else 0, PER, one, 0)
+            pick_tokens(c)
+        if DP == 2:
+            send_rows(c, 0)
+        if c == 0:
+            gate_tables()
+            loads[3].wait()
+        pick_cotangents(c)
+        send_rows(c, DP - 1)
+
+    def wait_rows(c, q):
+        def one(k, carry):
+            block = rows_part(recv.at[c, k], q, DP)
+            pltpu.make_async_copy(block, block, d_recv.at[c, q, k]).wait()
+            return carry
+
+        lax.fori_loop(0, PER, one, 0)
 
     def wait_dispatch(c):
-        def one(k, carry):
-            pltpu.make_async_copy(recv.at[c, k], recv.at[c, k], d_recv.at[c, k]).wait()
-            return carry
-
-        lax.fori_loop(0, PER, one, 0)
+        pass
 
     def products(c):
         if c == 0:
             load1.wait()
             load2.wait()
-        tok_rows = recv[c, :, 0].reshape(ROWS, width)
-        cot_rows = recv[c, :, 1].reshape(ROWS, width)
+        wait_rows(c, 0)
         tile = 512
 
         def hidden_tile(n, carry):
@@ -266,6 +299,12 @@
             return carry
 
         lax.fori_loop(0, 2 * half // tile, hidden_tile, 0)
+        if XP == 3:
+            for q in range(2):
+                for i in range(1, NX):
+                    scatter_copy(c, i, q).start()
+        if DP == 2:
+            wait_rows(c, 1)
 
         def act_tile(n, carry):
             at = pl.ds(pl.multiple_of(n * tile, tile), tile)
@@ -276,21 +315,25 @@
             return carry
 
         lax.fori_loop(0, half // tile, act_tile, 0)
-        for i in range(1, NX):
-            scatter_copy(c, i).start()
+        for q in range(2 if XP == 3 else 0, XP):
+            for i in range(1, NX):
+                scatter_copy(c, i, q).start()
 
     def reduce_x(c):
-        for i in range(1, NX):
-            scatter_copy(c, i).wait_recv()
+        for q in range(XP):
+            for i in range(1, NX):
+                scatter_copy(c, i, q).wait_recv()
         own = part[c, pl.ds(pl.multiple_of(x * QUART, QUART), QUART)].astype(F32)
         total = own + xrecv[c, 0].astype(F32)
         total += xrecv[c, 1].astype(F32)
         total += xrecv[c, 2].astype(F32)
         zsend[c] = total.astype(BF16)
-        exchange_copy(c).start()
+        for q in range(ZP):
+            exchange_copy(c, q).start()
 
     def activate(c):
-        exchange_copy(c).wait_recv()
+        for q in range(ZP):
+            exchange_copy(c, q).wait_recv()
         total = zsend[c].astype(F32) + zrecv[c].astype(F32)
         gate = total[:, :half]
         up = total[:, half : 2 * half]
@@ -303,23 +346,30 @@
             grad * up * sig * (1.0 + gate * (1.0 - sig))
         ).astype(BF16)
         act[c, block, 2 * half :] = (grad * silu).astype(BF16)
-        for i in range(1, NX):
-            gather_copy(c, i, x).start()
+        for q in range(AP):
+            for i in range(1, NX):
+                gather_copy(c, i, x, q).start()
 
     def results(c):
-        for i in range(1, NX):
-            gather_copy(c, i, (x + NX - i) % NX).wait_recv()
+        for q in range(AP):
+            for i in range(1, NX):
+                gather_copy(c, i, (x + NX - i) % NX, q).wait_recv()
         out = jnp.dot(act[c, :, 0:half], w2[...], preferred_element_type=F32)
         rsend[c, :, 0] = out.astype(BF16).reshape(PER, SLOTS, width)
+        if RP == 2:
+            send_results(c, 0)
         out = lax.dot_general(
             act[c, :, half:], w1[...], LAST, preferred_element_type=F32
         )
         rsend[c, :, 1] = out.astype(BF16).reshape(PER, SLOTS, width)
+        send_results(c, RP - 1)
+
+    def send_results(c, q):
         if c == 0:
-            own_return().start()
+            own_return(q).start()
 
         def one(j, carry):
-            return_copy(c, j).start()
+            return_copy(c, j, q).start()
             return carry
 
         lax.fori_loop(1 if c == 0 else 0, PER, one, 0)
@@ -331,7 +381,9 @@
 
     def combine(c):
         def arrived(k, carry):
-            pltpu.make_async_copy(rrecv.at[c, k], rrecv.at[c, k], r_recv.at[c, k]).wait()
+            for q in range(RP):
+                block = rows_part(rrecv.at[c, k], q, RP)
+                pltpu.make_async_copy(block, block, r_recv.at[c, q, k]).wait()
             return carry
 
         lax.fori_loop(0, PER, arrived, 0)
@@ -352,8 +404,7 @@
             tgrad_ref[...] = grads.astype(BF16)
 
     loads[2].wait()
-    loads[3].wait()
-    pick(0)
+    pick_tokens(0)
     pl.semaphore_wait(barrier, EXPERTS - 1 + NX)
 
     run = {
@@ -403,22 +454,33 @@
     for c in range(CHUNKS):
 
         def left(j, carry):
-            dispatch_copy(c, j).wait_send()
-            return_copy(c, j).wait_send()
+            for q in range(DP):
+                dispatch_copy(c, j, q).wait_send()
+            for q in range(RP):
+                return_copy(c, j, q).wait_send()
             return carry
 
         lax.fori_loop(1 if c == 0 else 0, PER, left, 0)
         for i in range(1, NX):
-            scatter_copy(c, i).wait_send()
-            gather_copy(c, i, x).wait_send()
-        exchange_copy(c).wait_send()
+            for q in range(XP):
+                scatter_copy(c, i, q).wait_send()
+            for q in range(AP):
+                gather_copy(c, i, x, q).wait_send()
+        for q in range(ZP):
+            exchange_copy(c, q).wait_send()
 
 
 def store_kernel(*refs):
     ins, outs, sem = refs[:4], refs[4:8], refs[8]
-    copies = [
-        pltpu.make_async_copy(ins[i], outs[i], sem.at[i]) for i in range(4)
-    ]
+    copies = []
+    for ref, out in zip(ins, outs):
+        parts = STORES if ref.shape[0] > ins[0].shape[0] else 1
+        rows = ref.shape[0] // parts
+        for n in range(parts):
+            at = pl.ds(n * rows, rows)
+            copies.append(
+                pltpu.make_async_copy(ref.at[at], out.at[at], sem.at[len(copies)])
+            )
     for copy in copies:
         copy.start()
     for copy in copies:
@@ -466,16 +528,16 @@
             pltpu.VMEM((toks, width), F32),
             pltpu.VMEM((toks, width), F32),
             dma((6,)),
-            dma((CHUNKS, PER)),
-            dma((CHUNKS, PER)),
-            dma((CHUNKS, NX - 1)),
-            dma((CHUNKS, NX - 1)),
-            dma((CHUNKS,)),
-            dma((CHUNKS,)),
-            dma((CHUNKS, NX - 1)),
-            dma((CHUNKS, NX - 1)),
-            dma((CHUNKS, PER)),
-            dma((CHUNKS, PER)),
+            dma((CHUNKS, DP, PER)),
+            dma((CHUNKS, DP, PER)),
+            dma((CHUNKS, NX - 1, XP)),
+            dma((CHUNKS, NX - 1, XP)),
+            dma((CHUNKS, ZP)),
+            dma((CHUNKS, ZP)),
+            dma((CHUNKS, NX - 1, AP)),
+            dma((CHUNKS, NX - 1, AP)),
+            dma((CHUNKS, RP, PER)),
+            dma((CHUNKS, RP, PER)),
         ],
         compiler_params=pltpu.CompilerParams(
             collective_id=0, has_side_effects=True, vmem_limit_bytes=VMEM_LIMIT
@@ -500,7 +562,7 @@
         out_shape=[jax.ShapeDtypeStruct(shape, BF16) for shape in shapes],
         in_specs=[vmem] * 4,
         out_specs=[hbm] * 4,
-        scratch_shapes=[dma((4,))],
+        scratch_shapes=[dma((2 + 2 * STORES,))],
         compiler_params=pltpu.CompilerParams(vmem_limit_bytes=2**20),
     )(*made)
     return mixed, token_grad, hidden_grad[None], output_grad[None]

time: 136 us -> 131 us (0.963)
  the two profiles are of different devices: /device:TPU:97 before, /device:TPU:1 now
where the time goes in v2:
time: 131 us
  Pallas kernels  130 us (99%)
    pallas_call x1, Pallas kernels, body(): pl.pallas_call(kernel, name='moe_layer', out_shape=[pltpu.VMEM(shape, BF1...  127 us
    pallas_call x1, Pallas kernels, body(): pl.pallas_call(store_kernel, name='store', out_shape=[jax.ShapeDtypeStruc...  2.78 us

profile of v2, /device:TPU:1, one launch (start us, length us, event | category | flops | bytes accessed | tf_op | source)
XLA Modules:
  0.0 130.9 jit_solution(12786642356539911809)
XLA Ops:
  0.6 127.3 %moe_layer.1 = (bf16[256,896]{1,0:T(8,128)(2,1)S(1)}, bf16[256,896]{1,0:T(8,128)(2,1)S(1)}, bf16[896,2048]{1,0:T(8,128)(2,1)S(1)}, bf16[1024,896]{1,0:T(8,128)(2,1)S(1)}) custom-call(s32[8,256]{1,0:T(8,128)} %bitcast.8, f32[8,256]{1,0:T(8,128)} %bitcast.9, bf16[256,896]{1,0:T(8,128)(2,1)} %tok_hbm.1, bf16[256,896]{1,0:T(8,128)(2,1)} %cot_hbm.1, ...), custom_call_target="tpu_custom_call" | custom-call | tf_op jit(solution)/shard_map/moe_layer/pallas_call | solution.py:499
  128.0 2.8 %store.1 = (bf16[256,896]{1,0:T(8,128)(2,1)}, bf16[256,896]{1,0:T(8,128)(2,1)}, bf16[896,2048]{1,0:T(8,128)(2,1)}, bf16[1024,896]{1,0:T(8,128)(2,1)}) custom-call(bf16[256,896]{1,0:T(8,128)(2,1)S(1)} %get-tuple-element.12.refs_0_, bf16[256,896]{1,0:T(8,128)(2,1)S(1)} %get-tuple-element.13.refs_1_, bf16[896,2048]{1,0:T(8,128)(2,1)S(1)} %get-tuple-element.14.refs_2_, ...), custom_call_target="tpu_custom_call" | custom-call | tf_op jit(solution)/shard_map/store/pallas_call | solution.py:559

commit v3 on v2

--- a/solution.py
+++ b/solution.py
@@ -19,16 +19,15 @@
 NX = 4
 QUART = ROWS // NX
 VMEM_LIMIT = 40 * 2**20
-STORES = 4
 XP = 1
-ZP = 3
+ZP = 1
 AP = 1
 DP = 2
 RP = 1
 LAST = (((1,), (1,)), ((), ()))
 FIRST = (((0,), (0,)), ((), ()))
 
-SCHEDULE = ('D0', 'D1', 'D2', 'D3', 'D4', 'D5', 'D6', 'D7', 'd0', 'p0', 't0', 'd1', 'p1', 'r0', 'd2', 'p2', 'r1', 'z0', 'd3', 'p3', 'r2', 'z1', 'g0', 'd4', 'p4', 'r3', 'z2', 'g1', 'd5', 'p5', 'r4', 'z3', 'g2', 'd6', 'p6', 'r5', 'z4', 'g3', 'd7', 'p7', 'r6', 'z5', 'g4', 'r7', 'z6', 'g5', 'z7', 'g6', 'g7', 'o0', 'h0', 'c0', 'c1', 'c2', 'c3', 'c4', 'c5', 'c6', 'c7')
+SCHEDULE = ('D0', 'D1', 'D2', 'D3', 'D4', 'D5', 'D6', 'D7', 'd0', 'p0', 't0', 'd1', 'p1', 'r0', 'd2', 'p2', 'r1', 'z0', 'd3', 'p3', 'r2', 'z1', 'g0', 'd4', 'p4', 'r3', 'z2', 'g1', 'd5', 'p5', 'r4', 'z3', 'g2', 'd6', 'p6', 'r5', 'z4', 'g3', 'd7', 'p7', 'r6', 'z5', 'g4', 'r7', 'z6', 'g5', 'z7', 'g6', 'g7', 'o0', 'h0', 'c0', 'c1', 'c2', 'c3', 'c4', 'c5', 'l0', 'c6', 'a0')
 
 
 def kernel(
@@ -38,10 +37,12 @@
     cot_hbm,
     w1_hbm,
     w2_hbm,
-    mixed_ref,
-    tgrad_ref,
+    mixed_sum,
+    grad_sum,
     hgrad_ref,
     ograd_ref,
+    last_rows,
+    last_tables,
     routing_ref,
     gate_ref,
     tok_ref,
@@ -64,8 +65,6 @@
     place_t,
     whi_t,
     wlo_t,
-    mixed_sum,
-    grad_sum,
     w_sem,
     d_send,
     d_recv,
@@ -146,10 +145,15 @@
     rank = jnp.dot(member.astype(BF16), earlier, preferred_element_type=F32)
     rank = jnp.where(member > 0.0, rank, -1.0).astype(BF16)
     slots = EXPERTS * SLOTS
-    order = lax.broadcasted_iota(jnp.int32, (slots, EXPERTS), 0) >> 4
-    spread = target(order // PER, order % PER) == lax.broadcasted_iota(
-        jnp.int32, (slots, EXPERTS), 1
-    )
+    ids = lax.broadcasted_iota(jnp.int32, (1, EXPERTS), 1)
+    place_of = (y + 4 - ((ids >> 1) & 3)) & 3
+    if SPLIT == 2:
+        place_of = (place_of * 2 + ((core + ids) & 1)) * PER + (ids >> 3)
+    else:
+        place_of = place_of * PER + (ids >> 3) * 2 + (ids & 1)
+    spread = (
+        lax.broadcasted_iota(jnp.int32, (slots, EXPERTS), 0) >> 4
+    ) == place_of
     spread = jnp.where(spread, 1.0, 0.0).astype(BF16)
     within = lax.broadcasted_iota(jnp.int32, (slots, toks), 0) & (SLOTS - 1)
     hits = jnp.dot(spread, rank, preferred_element_type=F32) == within.astype(F32)
@@ -379,7 +383,7 @@
         whi_t[...] = whi[...].T
         wlo_t[...] = wlo[...].T
 
-    def combine(c):
+    def wait_results(c):
         def arrived(k, carry):
             for q in range(RP):
                 block = rows_part(rrecv.at[c, k], q, RP)
@@ -387,6 +391,9 @@
             return carry
 
         lax.fori_loop(0, PER, arrived, 0)
+
+    def combine(c):
+        wait_results(c)
         at = pl.ds(c * ROWS, ROWS)
         back = rrecv[c, :, 0].reshape(ROWS, width)
         mixed = jnp.dot(whi_t[:, at], back, preferred_element_type=F32)
@@ -396,12 +403,18 @@
         if c > 0:
             mixed += mixed_sum[...]
             grads += grad_sum[...]
-        if c < CHUNKS - 1:
-            mixed_sum[...] = mixed
-            grad_sum[...] = grads
-        else:
-            mixed_ref[...] = mixed.astype(BF16)
-            tgrad_ref[...] = grads.astype(BF16)
+        mixed_sum[...] = mixed
+        grad_sum[...] = grads
+
+    def hand_over(_):
+        at = pl.ds((CHUNKS - 1) * ROWS, ROWS)
+        for n, table in enumerate((whi_t, wlo_t, place_t)):
+            last_tables[n] = table[:, at]
+
+    def last_arrivals(_):
+        wait_results(CHUNKS - 1)
+        for q in range(2):
+            last_rows[q] = rrecv[CHUNKS - 1, :, q].reshape(ROWS, width)
 
     loads[2].wait()
     pick_tokens(0)
@@ -448,6 +461,8 @@
     run["o"] = output_gradient
     run["h"] = hidden_gradient
     run["c"] = combine
+    run["l"] = hand_over
+    run["a"] = last_arrivals
     for step in SCHEDULE:
         run[step[0]](int(step[1]))
 
@@ -470,19 +485,32 @@
             exchange_copy(c, q).wait_send()
 
 
-def store_kernel(*refs):
-    ins, outs, sem = refs[:4], refs[4:8], refs[8]
-    copies = []
-    for ref, out in zip(ins, outs):
-        parts = STORES if ref.shape[0] > ins[0].shape[0] else 1
-        rows = ref.shape[0] // parts
-        for n in range(parts):
-            at = pl.ds(n * rows, rows)
-            copies.append(
-                pltpu.make_async_copy(ref.at[at], out.at[at], sem.at[len(copies)])
-            )
-    for copy in copies:
-        copy.start()
+def store_kernel(
+    mixed_sum,
+    grad_sum,
+    hgrad,
+    ograd,
+    rows,
+    tables,
+    mixed_out,
+    tgrad_out,
+    hgrad_out,
+    ograd_out,
+    mixed,
+    tgrad,
+    sem,
+):
+    pairs = ((hgrad, hgrad_out), (ograd, ograd_out), (mixed, mixed_out), (tgrad, tgrad_out))
+    copies = [pltpu.make_async_copy(*pair, sem.at[i]) for i, pair in enumerate(pairs)]
+    copies[0].start()
+    copies[1].start()
+    total = mixed_sum[...] + jnp.dot(tables[0], rows[0], preferred_element_type=F32)
+    total += jnp.dot(tables[1], rows[0], preferred_element_type=F32)
+    mixed[...] = total.astype(BF16)
+    copies[2].start()
+    total = grad_sum[...] + jnp.dot(tables[2], rows[1], preferred_element_type=F32)
+    tgrad[...] = total.astype(BF16)
+    copies[3].start()
     for copy in copies:
         copy.wait()
 
@@ -499,9 +527,11 @@
     made = pl.pallas_call(
         kernel,
         name="moe_layer",
-        out_shape=[pltpu.VMEM(shape, BF16) for shape in shapes],
+        out_shape=[pltpu.VMEM(shape, F32) for shape in shapes[:2]]
+        + [pltpu.VMEM(shape, BF16) for shape in shapes[2:]]
+        + [pltpu.VMEM((2, ROWS, width), BF16), pltpu.VMEM((3, toks, ROWS), BF16)],
         in_specs=[hbm] * 6,
-        out_specs=[vmem] * 4,
+        out_specs=[vmem] * 6,
         scratch_shapes=[
             pltpu.VMEM(routing.shape[::-1], jnp.int32),
             pltpu.VMEM(routing.shape[::-1], F32),
@@ -525,8 +555,6 @@
             pltpu.VMEM((toks, slots), BF16),
             pltpu.VMEM((toks, slots), BF16),
             pltpu.VMEM((toks, slots), BF16),
-            pltpu.VMEM((toks, width), F32),
-            pltpu.VMEM((toks, width), F32),
             dma((6,)),
             dma((CHUNKS, DP, PER)),
             dma((CHUNKS, DP, PER)),
@@ -560,10 +588,14 @@
         store_kernel,
         name="store",
         out_shape=[jax.ShapeDtypeStruct(shape, BF16) for shape in shapes],
-        in_specs=[vmem] * 4,
+        in_specs=[vmem] * 6,
         out_specs=[hbm] * 4,
-        scratch_shapes=[dma((2 + 2 * STORES,))],
-        compiler_params=pltpu.CompilerParams(vmem_limit_bytes=2**20),
+        scratch_shapes=[
+            pltpu.VMEM((toks, width), BF16),
+            pltpu.VMEM((toks, width), BF16),
+            dma((4,)),
+        ],
+        compiler_params=pltpu.CompilerParams(vmem_limit_bytes=8 * 2**20),
     )(*made)
     return mixed, token_grad, hidden_grad[None], output_grad[None]
 

time: 131 us -> 130 us (level)
  no operation moved by 1% of the time
where the time goes in v3:
time: 130 us
  Pallas kernels  129 us (99%)
    pallas_call x1, Pallas kernels, body(): pl.pallas_call(kernel, name='moe_layer', out_shape=[pltpu.VMEM(shape, F32...  126 us
    pallas_call x1, Pallas kernels, body(): pl.pallas_call(store_kernel, name='store', out_shape=[jax.ShapeDtypeStruc...  2.76 us

profile of v3, /device:TPU:1, one launch (start us, length us, event | category | flops | bytes accessed | tf_op | source)
XLA Modules:
  0.0 130.0 jit_solution(12911649705205188420)
XLA Ops:
  0.6 126.5 %moe_layer.1 = (f32[256,896]{1,0:T(8,128)S(1)}, f32[256,896]{1,0:T(8,128)S(1)}, bf16[896,2048]{1,0:T(8,128)(2,1)S(1)}, bf16[1024,896]{1,0:T(8,128)(2,1)S(1)}, bf...) custom-call(s32[8,256]{1,0:T(8,128)} %bitcast.8, f32[8,256]{1,0:T(8,128)} %bitcast.9, ...), custom_call_target="tpu_custom_call" | custom-call | tf_op jit(solution)/shard_map/moe_layer/pallas_call | solution.py:527
  127.1 2.8 %store.1 = (bf16[256,896]{1,0:T(8,128)(2,1)}, bf16[256,896]{1,0:T(8,128)(2,1)}, bf16[896,2048]{1,0:T(8,128)(2,1)}, bf16[1024,896]{1,0:T(8,128)(2,1)}) custom-call(f32[256,896]{1,0:T(8,128)S(1)} %get-tuple-element.14.mixed_sum, f32[256,896]{1,0:T(8,128)S(1)} %get-tuple-element.15.grad_sum, bf16[896,2048]{1,0:T(8,128)(2,1)S(1)} %get-tuple-element.16.hgrad, ...), custom_call_target="tpu_custom_call" | custom-call | tf_op jit(solution)/shard_map/store/pallas_call | solution.py:587

commit v4 on v3

--- a/solution.py
+++ b/solution.py
@@ -65,6 +65,7 @@
     place_t,
     whi_t,
     wlo_t,
+    ready,
     w_sem,
     d_send,
     d_recv,
@@ -124,7 +125,13 @@
     lax.fori_loop(1, EXPERTS, greet, 0)
     for i in range(1, NX):
         pl.semaphore_signal(barrier, inc=1, device_id=(x_peer(i), me), device_id_type=MESH)
-    pl.semaphore_signal(barrier, inc=1, device_id=(z_peer, me), device_id_type=MESH)
+
+    @pl.when(zh == 0)
+    def greet_upper():
+        pl.semaphore_signal(
+            barrier, inc=1, device_id=(z_peer, me), device_id_type=MESH
+        )
+
 
     load1.start()
     load2.start()
@@ -324,6 +331,12 @@
                 scatter_copy(c, i, q).start()
 
     def reduce_x(c):
+        if c == 0:
+
+            @pl.when(zh == 0)
+            def upper_is_in():
+                pl.semaphore_wait(ready, 1)
+
         for q in range(XP):
             for i in range(1, NX):
                 scatter_copy(c, i, q).wait_recv()
@@ -418,7 +431,12 @@
 
     loads[2].wait()
     pick_tokens(0)
-    pl.semaphore_wait(barrier, EXPERTS - 1 + NX)
+    pl.semaphore_wait(barrier, EXPERTS - 1 + NX - 1 + zh)
+
+    @pl.when(zh == 1)
+    def answer():
+        pl.semaphore_signal(ready, inc=1, device_id=(z_peer, me), device_id_type=MESH)
+
 
     run = {
         "D": start_dispatch,
@@ -555,6 +573,7 @@
             pltpu.VMEM((toks, slots), BF16),
             pltpu.VMEM((toks, slots), BF16),
             pltpu.VMEM((toks, slots), BF16),
+            pltpu.SemaphoreType.REGULAR,
             dma((6,)),
             dma((CHUNKS, DP, PER)),
             dma((CHUNKS, DP, PER)),

time: 130 us -> 129 us (level)
    pallas_call x1, Pallas kernels: 126 us -> 125 us  [body(): pl.pallas_call(kernel, name='moe_layer', out_shape=[pltpu.VMEM(shape, F32...]
where the time goes in v4:
time: 129 us
  Pallas kernels  128 us (99%)
    pallas_call x1, Pallas kernels, body(): pl.pallas_call(kernel, name='moe_layer', out_shape=[pltpu.VMEM(shape, F32...  125 us
    pallas_call x1, Pallas kernels, body(): pl.pallas_call(store_kernel, name='store', out_shape=[jax.ShapeDtypeStruc...  2.76 us

profile of v4, /device:TPU:1, one launch (start us, length us, event | category | flops | bytes accessed | tf_op | source)
XLA Modules:
  0.0 128.5 jit_solution(14505847882855645151)
XLA Ops:
  0.6 124.9 %moe_layer.1 = (f32[256,896]{1,0:T(8,128)S(1)}, f32[256,896]{1,0:T(8,128)S(1)}, bf16[896,2048]{1,0:T(8,128)(2,1)S(1)}, bf16[1024,896]{1,0:T(8,128)(2,1)S(1)}, bf...) custom-call(s32[8,256]{1,0:T(8,128)} %bitcast.8, f32[8,256]{1,0:T(8,128)} %bitcast.9, ...), custom_call_target="tpu_custom_call" | custom-call | tf_op jit(solution)/shard_map/moe_layer/pallas_call | solution.py:545
  125.6 2.8 %store.1 = (bf16[256,896]{1,0:T(8,128)(2,1)}, bf16[256,896]{1,0:T(8,128)(2,1)}, bf16[896,2048]{1,0:T(8,128)(2,1)}, bf16[1024,896]{1,0:T(8,128)(2,1)}) custom-call(f32[256,896]{1,0:T(8,128)S(1)} %get-tuple-element.14.mixed_sum, f32[256,896]{1,0:T(8,128)S(1)} %get-tuple-element.15.grad_sum, bf16[896,2048]{1,0:T(8,128)(2,1)S(1)} %get-tuple-element.16.hgrad, ...), custom_call_target="tpu_custom_call" | custom-call | tf_op jit(solution)/shard_map/store/pallas_call | solution.py:606

commit v5 on v4

--- a/solution.py
+++ b/solution.py
@@ -16,6 +16,7 @@
 PER = EXPERTS // CHUNKS
 SPLIT = CHUNKS // 4
 ROWS = PER * SLOTS
+OWN = 6
 NX = 4
 QUART = ROWS // NX
 VMEM_LIMIT = 40 * 2**20
@@ -104,12 +105,12 @@
 
     def target(c, k):
         if SPLIT == 2:
-            return k * 8 + ((y + 4 - c // 2) % 4) * 2 + (core + c) % 2
+            return k * 8 + ((y + 3 - c // 2) % 4) * 2 + (core + c) % 2
         return (k // 2) * 8 + ((y + 4 - c) % 4) * 2 + k % 2
 
     def origin(c, k):
         if SPLIT == 2:
-            return k * 8 + ((y + c // 2) % 4) * 2 + (core + c) % 2
+            return k * 8 + ((y + 1 + c // 2) % 4) * 2 + (core + c) % 2
         return (k // 2) * 8 + ((y + c) % 4) * 2 + k % 2
 
     mine = zl if SPLIT == 2 else zl * 2 + core
@@ -153,7 +154,7 @@
     rank = jnp.where(member > 0.0, rank, -1.0).astype(BF16)
     slots = EXPERTS * SLOTS
     ids = lax.broadcasted_iota(jnp.int32, (1, EXPERTS), 1)
-    place_of = (y + 4 - ((ids >> 1) & 3)) & 3
+    place_of = (y + 3 - ((ids >> 1) & 3)) & 3
     if SPLIT == 2:
         place_of = (place_of * 2 + ((core + ids) & 1)) * PER + (ids >> 3)
     else:
@@ -207,9 +208,9 @@
 
     def own_dispatch(q):
         return pltpu.make_async_copy(
-            rows_part(send.at[0, mine], q, DP),
-            rows_part(recv.at[0, mine], q, DP),
-            d_recv.at[0, q, mine],
+            rows_part(send.at[OWN, mine], q, DP),
+            rows_part(recv.at[OWN, mine], q, DP),
+            d_recv.at[OWN, q, mine],
         )
 
     def return_copy(c, j, q):
@@ -226,9 +227,9 @@
 
     def own_return(q):
         return pltpu.make_async_copy(
-            rows_part(rsend.at[0, mine], q, RP),
-            rows_part(rrecv.at[0, mine], q, RP),
-            r_recv.at[0, q, mine],
+            rows_part(rsend.at[OWN, mine], q, RP),
+            rows_part(rrecv.at[OWN, mine], q, RP),
+            r_recv.at[OWN, q, mine],
         )
 
     def scatter_copy(c, i, q):
@@ -264,14 +265,14 @@
         )
 
     def send_rows(c, q):
-        if c == 0:
+        if c == OWN:
             own_dispatch(q).start()
 
         def one(j, carry):
             dispatch_copy(c, j, q).start()
             return carry
 
-        lax.fori_loop(1 if c == 0 else 0, PER, one, 0)
+        lax.fori_loop(1 if c == OWN else 0, PER, one, 0)
 
     def start_dispatch(c):
         if c > 0:
@@ -382,14 +383,14 @@
         send_results(c, RP - 1)
 
     def send_results(c, q):
-        if c == 0:
+        if c == OWN:
             own_return(q).start()
 
         def one(j, carry):
             return_copy(c, j, q).start()
             return carry
 
-        lax.fori_loop(1 if c == 0 else 0, PER, one, 0)
+        lax.fori_loop(1 if c == OWN else 0, PER, one, 0)
 
     def transposes():
         place_t[...] = place[...].T
@@ -493,7 +494,7 @@
                 return_copy(c, j, q).wait_send()
             return carry
 
-        lax.fori_loop(1 if c == 0 else 0, PER, left, 0)
+        lax.fori_loop(1 if c == OWN else 0, PER, left, 0)
         for i in range(1, NX):
             for q in range(XP):
                 scatter_copy(c, i, q).wait_send()

time: 129 us -> 128 us (level)
  no operation moved by 1% of the time
where the time goes in v5:
time: 128 us
  Pallas kernels  127 us (99%)
    pallas_call x1, Pallas kernels, body(): pl.pallas_call(kernel, name='moe_layer', out_shape=[pltpu.VMEM(shape, F32...  125 us
    pallas_call x1, Pallas kernels, body(): pl.pallas_call(store_kernel, name='store', out_shape=[jax.ShapeDtypeStruc...  2.76 us

profile of v5, /device:TPU:1, one launch (start us, length us, event | category | flops | bytes accessed | tf_op | source)
XLA Modules:
  0.0 128.2 jit_solution(951433328952266698)
XLA Ops:
  0.6 124.7 %moe_layer.1 = (f32[256,896]{1,0:T(8,128)S(1)}, f32[256,896]{1,0:T(8,128)S(1)}, bf16[896,2048]{1,0:T(8,128)(2,1)S(1)}, bf16[1024,896]{1,0:T(8,128)(2,1)S(1)}, bf...) custom-call(s32[8,256]{1,0:T(8,128)} %bitcast.8, f32[8,256]{1,0:T(8,128)} %bitcast.9, ...), custom_call_target="tpu_custom_call" | custom-call | tf_op jit(solution)/shard_map/moe_layer/pallas_call | solution.py:546
  125.3 2.8 %store.1 = (bf16[256,896]{1,0:T(8,128)(2,1)}, bf16[256,896]{1,0:T(8,128)(2,1)}, bf16[896,2048]{1,0:T(8,128)(2,1)}, bf16[1024,896]{1,0:T(8,128)(2,1)}) custom-call(f32[256,896]{1,0:T(8,128)S(1)} %get-tuple-element.14.mixed_sum, f32[256,896]{1,0:T(8,128)S(1)} %get-tuple-element.15.grad_sum, bf16[896,2048]{1,0:T(8,128)(2,1)S(1)} %get-tuple-element.16.hgrad, ...), custom_call_target="tpu_custom_call" | custom-call | tf_op jit(solution)/shard_map/store/pallas_call | solution.py:607
